TPU v7x, 256 devices: a whole 4x4x8 slice. The times are simulated.
256 devices in a mesh: rep: 4 (over x_lo, core), fsdp: 64 (over z, x_hi, y).
Axes of the slice: x: 4 (x_hi: 2, x_lo: 2; x = x_hi * 2 + x_lo), y: 4, z: 8, core: 2. Of those that a mesh axis runs over, the one named last changes fastest.
Arguments:
- tokens: bfloat16 [4096, 4096], P(('rep', 'fsdp')), may hold values from -6 to 6
- readout: bfloat16 [4096, 14336], P('rep', 'fsdp'), may hold values from -0.046875 to 0.046875
- resp_mask: int32 [4096], P('rep'), may hold values 0 or 1
- order: int32 [4, 64], P('rep'), may hold values from 0 to 63, each once within a row
- w_gate: bfloat16 [4, 14336, 4096], P('rep', 'fsdp'), may hold values from -0.09375 to 0.09375
- w_up: bfloat16 [4, 14336, 4096], P('rep', 'fsdp'), may hold values from -0.09375 to 0.09375
- outer_gate: bfloat16 [14336, 4096], P('fsdp', 'rep'), may hold values from -0.09375 to 0.09375
- outer_up: bfloat16 [14336, 4096], P('fsdp', 'rep'), may hold values from -0.09375 to 0.09375
- moment: float32 [14336, 4096], P('fsdp', 'rep'), may hold values from -0.09375 to 0.09375
Outputs:
- loss: float32 [4], P('rep')
- grad_gate: bfloat16 [4, 14336, 4096], P('rep', 'fsdp')
- grad_up: bfloat16 [4, 14336, 4096], P('rep', 'fsdp')
- new_outer: bfloat16 [14336, 4096], P('fsdp', 'rep')
- new_moment: float32 [14336, 4096], P('fsdp', 'rep')
Inputs may be any that keep to these rules, and one draw needn't show every extreme that they name: Each row of order holds every sequence number of its group once.
All inputs are finite; a program needn't handle non-finite values. Where the computation divides by a largest or mean magnitude, that divisor is 1e-20 or more. No bound on the sum of `resp_mask` on one device may be relied on, other than what follows from the above.
Results may differ from a plain program's by a relative error of at most 0.022.
Values may be sent and summed in bfloat16 or wider, within the bound.
A program may use at most 128 MiB of HBM per device.

v0:
```python
import jax
import jax.numpy as jnp
from jax import lax
from jax.sharding import PartitionSpec as P

BLOCK = 128
LEN = 16
dpo_beta = 0.1
outer_rate = 0.7
outer_mu = 0.9
tiny_eps = 1e-06


def project(rows, weight):
    return lax.dot_general(
        rows, weight, (((1,), (1,)), ((), ())), preferred_element_type=jnp.float32
    )


def local_scores(hidden, readout, mask_f, seqs):
    per_token = jnp.sum(hidden.astype(jnp.float32) * readout.astype(jnp.float32), axis=1)
    return jnp.sum((per_token * mask_f).reshape(seqs, LEN), axis=1)


def per_device(tokens, readout, resp_mask, order, w_gate, w_up, outer_gate, outer_up, moment):
    full_gate, full_up = (
        lax.all_gather(outer_gate, "rep", axis=1, tiled=True),
        lax.all_gather(outer_up, "rep", axis=1, tiled=True),
    )
    policy_gate = w_gate[0]
    policy_up = w_up[0]
    inputs = lax.all_gather(tokens, "fsdp", axis=0, tiled=True)
    gate = project(inputs, policy_gate)
    upper = project(inputs, policy_up)
    gate_ref = project(inputs, full_gate)
    upper_ref = project(inputs, full_up)
    group_tok = inputs.shape[0]
    seqs = group_tok // LEN
    mask_f = resp_mask.astype(jnp.float32)
    hidden = (jax.nn.silu(gate) * upper).astype(jnp.bfloat16)
    hidden_ref = (jax.nn.silu(gate_ref) * upper_ref).astype(jnp.bfloat16)
    score, score_ref = lax.psum(
        (
            local_scores(hidden, readout, mask_f, seqs),
            local_scores(hidden_ref, readout, mask_f, seqs),
        ),
        "fsdp",
    )
    places = jnp.arange(seqs, dtype=jnp.int32)
    pick_chosen = (order[0, 0::2][:, None] == places[None, :]).astype(jnp.float32)
    pick_rejected = (order[0, 1::2][:, None] == places[None, :]).astype(jnp.float32)
    relative = score - score_ref
    highest = lax.Precision.HIGHEST
    margin = dpo_beta * (
        jnp.dot(pick_chosen, relative, precision=highest)
        - jnp.dot(pick_rejected, relative, precision=highest)
    )
    loss = jnp.mean(jax.nn.softplus(-margin)).reshape(1)
    weight = dpo_beta * jax.nn.sigmoid(-margin) / pick_chosen.shape[0]
    coef = jnp.dot(weight, pick_rejected - pick_chosen, precision=highest)
    token_grad = jnp.broadcast_to(coef[:, None], (seqs, LEN)).reshape(-1) * mask_f
    hidden_grad = token_grad[:, None] * readout.astype(jnp.float32)
    sigma = jax.nn.sigmoid(gate)
    gate_grad = (hidden_grad * upper * sigma * (1.0 + gate * (1.0 - sigma))).astype(jnp.bfloat16)
    up_grad = (hidden_grad * jax.nn.silu(gate)).astype(jnp.bfloat16)
    contract = (((0,), (0,)), ((), ()))
    grad_gate = lax.dot_general(
        gate_grad, inputs, contract, preferred_element_type=jnp.float32
    ).astype(jnp.bfloat16)
    grad_up = lax.dot_general(up_grad, inputs, contract, preferred_element_type=jnp.float32).astype(
        jnp.bfloat16
    )
    unit_rows = full_gate.shape[0]
    delta = full_gate.astype(jnp.float32) - policy_gate.astype(jnp.float32)
    blocks = delta.reshape(unit_rows, -1, BLOCK)
    scale = (jnp.max(jnp.abs(blocks), axis=2, keepdims=True) + tiny_eps).astype(jnp.bfloat16)
    levels = (blocks / scale.astype(jnp.float32)).astype(jnp.bfloat16)
    groups = lax.axis_size("rep")
    terms = (levels.astype(jnp.float32) * scale.astype(jnp.float32)).reshape(unit_rows, -1)
    total = lax.psum_scatter(
        terms.astype(jnp.bfloat16), "rep", scatter_dimension=1, tiled=True
    ).astype(jnp.float32)
    average = total / groups
    new_moment = outer_mu * moment + average
    new_outer = (
        outer_gate.astype(jnp.float32) - outer_rate * (average + outer_mu * new_moment)
    ).astype(jnp.bfloat16)
    return (loss, grad_gate[None], grad_up[None], new_outer, new_moment)


def solution(mesh):
    return jax.shard_map(
        per_device,
        mesh=mesh,
        in_specs=(
            P(("rep", "fsdp"), None),
            P("rep", "fsdp"),
            P("rep"),
            P("rep", None),
            P("rep", "fsdp", None),
            P("rep", "fsdp", None),
            P("fsdp", "rep"),
            P("fsdp", "rep"),
            P("fsdp", "rep"),
        ),
        out_specs=(
            P("rep"),
            P("rep", "fsdp", None),
            P("rep", "fsdp", None),
            P("fsdp", "rep"),
            P("fsdp", "rep"),
        ),
        check_vma=False,
    )
```

profile of v0, /device:TPU:2, one launch (start us, length us, event | category | flops | bytes accessed | tf_op | source)
XLA Modules:
  0.0 466.0 jit_solution(16427178451897451544)
XLA Ops:
  8.0 0.0 copy-start
  8.0 0.0 all-gather.6.cloned.1.call-start
  8.1 0.7 all-gather.6.cloned.1.call-update
  8.7 0.0 reduce-scatter.2.cloned.1.call-start
  8.8 32.6 %all-gather.6.cloned.1.call-done = bf16[224,4096]{1,0:T(8,128)(2,1)} async-done(((bf16[224,1024]{1,0:T(8,128)(2,1)}), bf16[224,4096]{1,0:T(8,128)(2,1)}) %all-gather.6.cloned.1.call-update) | async-done | bytes 1835024 | tf_op jit(solution)/shard_map/all_gather | solution.py:27
  41.4 2.7 abs_bitcast_fusion
  44.2 2.4 copy.14
  46.6 3.1 reduce_max.9
  49.7 0.0 copy-start.1
  49.7 0.0 copy-start.2
  49.7 1.0 div.44
  50.7 0.5 copy-done.1
  51.2 0.6 copy-done.2
  51.7 0.0 copy-start.9
  51.7 0.0 copy-start.4
  51.7 0.0 copy-start.5
  51.7 4.3 fusion.3
  56.1 0.0 reduce-scatter.2.cloned.1.call-update
  56.1 0.0 all-gather.4.cloned.1.call-start
  56.1 0.5 all-gather.4.cloned.1.call-update
  56.7 0.2 all-gather.8.cloned.1.call-start
  56.9 0.4 all-gather.8.cloned.1.call-update
  57.3 0.0 copy-done.9
  57.3 0.1 slice.7
  57.4 0.1 slice.6
  57.5 29.5 %reduce-scatter.2.cloned.1.call-done = bf16[224,1024]{1,0:T(8,128)(2,1)} async-done(((bf16[224,4096]{1,0:T(8,128)(2,1)}), bf16[224,1024]{1,0:T(8,128)(2,1)}) %reduce-scatter.2.cloned.1.call-update) | async-done | bytes 458768 | tf_op jit(solution)/shard_map/reduce_scatter | solution.py:80
  87.0 0.0 copy-done.4
  87.0 0.0 copy-done.5
  87.0 2.4 subtract_convert_fusion
  89.4 125.4 %all-gather.4.cloned.1.call-done = bf16[1024,4096]{1,0:T(8,128)(2,1)} async-done(((bf16[16,4096]{1,0:T(8,128)(2,1)}), bf16[1024,4096]{1,0:T(8,128)(2,1)}) %all-gather.4.cloned.1.call-update) | async-done | bytes 8388624 | tf_op jit(solution)/shard_map/all_gather | solution.py:32
  214.9 0.0 copy-start.3
  214.9 0.0 copy-start.7
  214.9 7.6 %fusion.6 = f32[1024,224]{0,1:T(8,128)} fusion(bf16[1024,4096]{1,0:T(8,128)(2,1)} %all-gather.4.cloned.1.call-done, bf16[1,224,4096]{2,1,0:T(8,128)(2,1)} %param.13), kind=kOutput, calls=%fused_computation.12 | convolution fusion | flops 1879048192 | bytes 11141120 | tf_op jit(solution)/shard_map/dot_general | solution.py:15
  222.5 0.0 copy-done.3
  222.5 0.0 copy-done.7
  222.5 0.0 copy-start.8
  222.5 3.6 fusion.47
  226.1 16.0 %all-gather.8.cloned.1.call-done = bf16[224,4096]{1,0:T(8,128)(2,1)} async-done(((bf16[224,1024]{1,0:T(8,128)(2,1)}), bf16[224,4096]{1,0:T(8,128)(2,1)}) %all-gather.8.cloned.1.call-update) | async-done | bytes 1835024 | tf_op jit(solution)/shard_map/all_gather | solution.py:28
  242.1 0.0 copy-done.8
  242.1 0.0 copy-start.10
  242.1 7.1 %fusion.10 = f32[1024]{0:T(1024)S(1)} fusion(bf16[1024,224]{0,1:T(8,128)(2,1)S(1)} %copy-done.8, bf16[1024,4096]{1,0:T(8,128)(2,1)} %all-gather.4.cloned.1.call-done, bf16[224,4096]{1,0:T(8,128)(2,1)} %all-gather.8.cloned.1.call-done, f32[1024,224]{0,1:T(8,128)} %fusion.47), kind=kOutput, calls=%fused_computation.20 | convolution fusion | flops 1881340928 | bytes 11603968 | tf_op jit(solution)/shard_map/dot_general | solution.py:15
  249.2 0.0 copy-done
  249.2 0.0 copy-done.10
  249.2 0.0 copy-start.6
  249.2 7.1 %fusion.19 = (f32[1024]{0:T(1024)S(1)}, f32[1024,224]{0,1:T(8,128)}) fusion(bf16[1024,224]{0,1:T(8,128)(2,1)S(1)} %copy-done.8, f32[1024,224]{0,1:T(8,128)S(1)} %copy-done.10, bf16[1024,4096]{1,0:T(8,128)(2,1)} %all-gather.4.cloned.1.call-done, bf16[1,224,4096]{2,1,0:T(8,128)(2,1)S(1)} %copy-done), kind=kOutput, calls=%fused_computation.32 | convolution fusion | flops 1881340928 | bytes 12521472 | tf_op jit(solution)/shard_map/dot_general | solution.py:15
  256.3 0.0 copy-done.6
  256.4 0.1 reshape.40
  256.4 0.1 reshape.39
  256.5 0.1 reduce_sum.48
  256.6 0.1 reduce_sum.46
  256.7 184.5 %all-reduce = (f32[64]{0:T(128)S(1)}, f32[64]{0:T(128)S(1)}) all-reduce(f32[64]{0:T(128)S(1)} %reduce_sum.46, f32[64]{0:T(128)S(1)} %reduce_sum.48), channel_id=1, replica_groups=mesh['rep'=4,'fsdp'=64] {'fsdp'}, use_global_device_ids=true, to_apply=%region_2.3 | all-reduce | flops 128 | bytes 1024 | tf_op jit(solution)/shard_map/psum | solution.py:42
  441.2 0.2 convolution_bitcast_fusion.2
  441.4 0.8 fusion.35
  442.3 0.2 convolution_bitcast_fusion
  442.5 0.1 broadcast_in_dim.6
  442.5 0.1 reshape.42
  443.3 0.0 copy-start.11
  443.3 0.0 copy-start.12
  443.3 7.2 %fusion.1 = bf16[1,224,4096]{2,1,0:T(8,128)(2,1)} fusion(bf16[1024,4096]{1,0:T(8,128)(2,1)} %all-gather.4.cloned.1.call-done, bf16[1024,224]{0,1:T(8,128)(2,1)S(1)} %copy-done.8, f32[1024]{0:T(1024)S(1)} %convert_multiply_fusion.4, f32[1024,224]{0,1:T(8,128)} %fusion.6), kind=kOutput, calls=%fused_computation.3 | convolution fusion | flops 1881800704 | bytes 11603968 | tf_op jit(solution)/shard_map/dot_general | solution.py:70
  450.5 0.0 copy-done.11
  450.5 0.0 copy-done.12
  450.5 6.9 %fusion = bf16[1,224,4096]{2,1,0:T(8,128)(2,1)} fusion(bf16[1024,4096]{1,0:T(8,128)(2,1)} %all-gather.4.cloned.1.call-done, f32[1024,224]{0,1:T(8,128)S(1)} %copy-done.12, bf16[1024,224]{0,1:T(8,128)(2,1)S(1)} %copy-done.8, f32[1024,224]{0,1:T(8,128)S(1)} %copy-done.11, f32[1024]{0:T(1024)S(1)} %convert_multiply_fusion.4), kind=kOutput, calls=%fused_computation.2 | convolution fusion | flops 1882718208 | bytes 12521472 | tf_op jit(solution)/shard_map/dot_general | solution.py:67
  (3 shorter events, 0.0 us)
Async XLA Ops:
  8.0 241.2 %copy-start = (bf16[1,224,4096]{2,1,0:T(8,128)(2,1)S(1)}, bf16[1,224,4096]{2,1,0:T(8,128)(2,1)}, u32[]{:S(2)}) copy-start(bf16[1,224,4096]{2,1,0:T(8,128)(2,1)} %param.14) | copy-start | bytes 5505028
  8.0 33.4 %all-gather.6.cloned.1.call-start = ((), (), s32[]{:S(2)}) async-start(), calls=%async_computation.2 | async-start | bytes 2293760 | tf_op jit(solution)/shard_map/all_gather | solution.py:27
  8.7 78.3 %reduce-scatter.2.cloned.1.call-start = ((), (), s32[]{:S(2)}) async-start(), calls=%async_computation.4 | async-start | bytes 2293760 | tf_op jit(solution)/shard_map/reduce_scatter | solution.py:80
  49.7 1.5 copy-start.1
  49.7 2.0 copy-start.2
  51.7 5.5 %copy-start.9 = (s32[1,64]{1,0:T(1,128)S(1)}, s32[1,64]{1,0:T(1,128)}, u32[]{:S(2)}) copy-start(s32[1,64]{1,0:T(1,128)} %param.12) | copy-start | bytes 772
  51.7 35.3 %copy-start.4 = (bf16[224,1024]{1,0:T(8,128)(2,1)S(1)}, bf16[224,1024]{1,0:T(8,128)(2,1)}, u32[]{:S(2)}) copy-start(bf16[224,1024]{1,0:T(8,128)(2,1)} %param.15) | copy-start | bytes 1376260
  51.7 35.3 %copy-start.5 = (f32[224,1024]{1,0:T(8,128)S(1)}, f32[224,1024]{1,0:T(8,128)}, u32[]{:S(2)}) copy-start(f32[224,1024]{1,0:T(8,128)} %param.17) | copy-start | bytes 2752516
  56.1 158.8 %all-gather.4.cloned.1.call-start = ((), (), s32[]{:S(2)}) async-start(), calls=%async_computation.1 | async-start | bytes 8519680 | tf_op jit(solution)/shard_map/all_gather | solution.py:32
  56.7 185.4 %all-gather.8.cloned.1.call-start = ((), (), s32[]{:S(2)}) async-start(), calls=%async_computation.3 | async-start | bytes 2293760 | tf_op jit(solution)/shard_map/all_gather | solution.py:28
  214.9 7.6 %copy-start.3 = (bf16[224,4096]{1,0:T(8,128)(2,1)S(1)}, bf16[224,4096]{1,0:T(8,128)(2,1)}, u32[]{:S(2)}) copy-start(bf16[224,4096]{1,0:T(8,128)(2,1)} %all-gather.6.cloned.1.call-done) | copy-start | bytes 5505028
  214.9 7.6 %copy-start.7 = (bf16[1024,4096]{1,0:T(8,128)(2,1)S(1)}, bf16[1024,4096]{1,0:T(8,128)(2,1)}, u32[]{:S(2)}) copy-start(bf16[1024,4096]{1,0:T(8,128)(2,1)} %all-gather.4.cloned.1.call-done) | copy-start | bytes 25165828
  222.5 19.6 %copy-start.8 = (bf16[1024,224]{0,1:T(8,128)(2,1)S(1)}, bf16[1024,224]{0,1:T(8,128)(2,1)}, u32[]{:S(2)}) copy-start(bf16[1024,224]{0,1:T(8,128)(2,1)} %param.10) | copy-start | bytes 1376260
  242.1 7.1 %copy-start.10 = (f32[1024,224]{0,1:T(8,128)S(1)}, f32[1024,224]{0,1:T(8,128)}, u32[]{:S(2)}) copy-start(f32[1024,224]{0,1:T(8,128)} %fusion.6) | copy-start | bytes 2752516
  249.2 7.2 %copy-start.6 = (s32[1024]{0:T(1024)S(1)}, s32[1024]{0:T(1024)}, u32[]{:S(2)}) copy-start(s32[1024]{0:T(1024)} %param.11) | copy-start | bytes 12292
  443.3 7.2 %copy-start.11 = (f32[1024,224]{0,1:T(8,128)S(1)}, f32[1024,224]{0,1:T(8,128)}, u32[]{:S(2)}) copy-start(f32[1024,224]{0,1:T(8,128)} %fusion.6) | copy-start | bytes 2752516
  443.3 7.2 %copy-start.12 = (f32[1024,224]{0,1:T(8,128)S(1)}, f32[1024,224]{0,1:T(8,128)}, u32[]{:S(2)}) copy-start(f32[1024,224]{0,1:T(8,128)} %get-tuple-element.12) | copy-start | bytes 2752516
Sparse Core Ops, SparseCore 0:
  10.7 30.7 all-gather.5
  56.2 30.7 reduce-scatter.1
Sparse Core Ops, SparseCore 1:
  60.1 154.7 all-gather.3
  216.5 25.5 all-gather.7
where the time goes:
time: 466 us
  waiting for transfers between devices  205 us (44%)
  blocking collectives  185 us (40%)
  matrix products  40.7 us (9%)
  between operations  17.4 us (4%)
  other arithmetic  12.8 us (3%)
  local copies, waits for them, and re-layouts  5.06 us (1%)
    psum x1, blocking collectives, per_device(): lax.psum((local_scores(hidden, readout, mask_f, seqs), local_scores(hidde...  185 us
    all_gather x1, waiting for transfers between devices, per_device(): inputs = lax.all_gather(tokens, 'fsdp', axis=0, tiled=True)  125 us
    all_gather x1, waiting for transfers between devices, per_device(): lax.all_gather(outer_gate, 'rep', axis=1, tiled=True)  32.6 us
    reduce_scatter x1, waiting for transfers between devices, per_device(): lax.psum_scatter(terms.astype(jnp.bfloat16), 'rep', scatter_dimension=1,...  29.5 us
    dot_general x4, matrix products, project(): lax.dot_general(rows, weight, (((1,), (1,)), ((), ())), preferred_element...  25.4 us
    all_gather x1, waiting for transfers between devices, per_device(): lax.all_gather(outer_up, 'rep', axis=1, tiled=True)  16 us
  transfers between devices with their start and end apart: 4, of which 4 were waited for; matrix products, arithmetic and copies ran while one was open for 3% of the time, Pallas kernels for 0%

commit v1 on v0

--- a/solution.py
+++ b/solution.py
@@ -9,6 +9,13 @@
 outer_rate = 0.7
 outer_mu = 0.9
 tiny_eps = 1e-06
+
+
+def gather_over(x, name, d):
+    peers = lax.axis_size(name)
+    blocks = jnp.stack([x for _ in range(peers)])
+    blocks = lax.all_to_all(blocks, name, split_axis=0, concat_axis=0)
+    return jnp.concatenate(blocks, axis=d)
 
 
 def project(rows, weight):
@@ -29,7 +36,7 @@
     )
     policy_gate = w_gate[0]
     policy_up = w_up[0]
-    inputs = lax.all_gather(tokens, "fsdp", axis=0, tiled=True)
+    inputs = gather_over(tokens, "fsdp", 0)
     gate = project(inputs, policy_gate)
     upper = project(inputs, policy_up)
     gate_ref = project(inputs, full_gate)

time: 466 us -> 447 us (0.959)
  waiting for transfers between devices: 205 us -> 167 us
  starting transfers between devices: 0.34 us -> 14.2 us
  local copies, waits for them, and re-layouts: 5.06 us -> 10.4 us
    all_gather x1 -> x0, waiting for transfers between devices: 125 us -> none  [per_device(): inputs = lax.all_gather(tokens, 'fsdp', axis=0, tiled=True)]
    all_to_all x0 -> x1, waiting for transfers between devices: none -> 64.6 us  [gather_over(): blocks = lax.all_to_all(blocks, name, split_axis=0, concat_axis=0)]
    reduce_scatter x1, waiting for transfers between devices: 29.5 us -> 51.1 us  [per_device(): lax.psum_scatter(terms.astype(jnp.bfloat16), 'rep', scatter_dimension=1,...]
    all_gather x1, waiting for transfers between devices: 32.6 us -> 50.6 us  [per_device(): lax.all_gather(outer_gate, 'rep', axis=1, tiled=True)]
    all_gather x1, waiting for transfers between devices: 16 us -> 0.01 us  [per_device(): lax.all_gather(outer_up, 'rep', axis=1, tiled=True)]
    all_to_all x0 -> x1, starting transfers between devices: none -> 13.9 us  [gather_over(): blocks = lax.all_to_all(blocks, name, split_axis=0, concat_axis=0)]
    another operation x0 -> x1, local copies, waits for them, and re-layouts: none -> 5.3 us  [gather_over(): blocks = jnp.stack([x for _ in range(peers)])]
  transfers between devices with their start and end apart: 4 -> 4, of which waited for: 4 -> 3; matrix products, arithmetic and copies ran while one was open for 3% -> 8% of each run, Pallas kernels for 0% -> 0%
where the time goes in v1:
time: 447 us; the launch traced here: 446 us
  blocking collectives  183 us (41%)
  waiting for transfers between devices  167 us (37%)
  matrix products  43.4 us (10%)
  between operations  15.7 us (4%)
  starting transfers between devices  14.2 us (3%)
  other arithmetic  12.8 us (3%)
  local copies, waits for them, and re-layouts  10.4 us (2%)
    psum x1, blocking collectives, per_device(): lax.psum((local_scores(hidden, readout, mask_f, seqs), local_scores(hidde...  183 us
    all_to_all x1, waiting for transfers between devices, gather_over(): blocks = lax.all_to_all(blocks, name, split_axis=0, concat_axis=0)  64.6 us
    reduce_scatter x1, waiting for transfers between devices, per_device(): lax.psum_scatter(terms.astype(jnp.bfloat16), 'rep', scatter_dimension=1,...  51.1 us
    all_gather x1, waiting for transfers between devices, per_device(): lax.all_gather(outer_gate, 'rep', axis=1, tiled=True)  50.6 us
    dot_general x4, matrix products, project(): lax.dot_general(rows, weight, (((1,), (1,)), ((), ())), preferred_element...  28.1 us
    all_to_all x1, starting transfers between devices, gather_over(): blocks = lax.all_to_all(blocks, name, split_axis=0, concat_axis=0)  13.9 us
  transfers between devices with their start and end apart: 4, of which 3 were waited for; matrix products, arithmetic and copies ran while one was open for 8% of the time, Pallas kernels for 0%

profile of v1, /device:TPU:2, one launch (start us, length us, event | category | flops | bytes accessed | tf_op | source)
XLA Modules:
  0.0 446.5 jit_solution(10966070103536224100)
XLA Ops:
  7.2 0.0 copy-start
  7.2 5.3 %stack.2 = bf16[64,16,4096]{2,1,0:T(8,128)(2,1)} broadcast(bf16[16,4096]{1,0:T(8,128)(2,1)} %param.9), dimensions={1,2} | broadcast | bytes 8519680 | tf_op jit(solution)/shard_map/stack | solution.py:16
  12.5 13.9 %all-to-all-start = ((bf16[64,16,4096]{2,1,0:T(8,128)(2,1)}), bf16[64,16,4096]{2,1,0:T(8,128)(2,1)}, u32[]{:S(2)}, u32[]{:S(2)}) async-start(bf16[64,16,4096]{2,1,0:T(8,128)(2,1)} %stack.2), calls=%async_computation | async-start | bytes 16777216 | tf_op jit(solution)/shard_map/all_to_all | solution.py:17
  26.4 0.0 all-gather.3.cloned.1.call-start
  26.5 0.7 all-gather.3.cloned.1.call-update
  27.2 0.0 reduce-scatter.2.cloned.1.call-start
  27.2 50.6 %all-gather.3.cloned.1.call-done = bf16[224,4096]{1,0:T(8,128)(2,1)} async-done(((bf16[224,1024]{1,0:T(8,128)(2,1)}), bf16[224,4096]{1,0:T(8,128)(2,1)}) %all-gather.3.cloned.1.call-update) | async-done | bytes 1835024 | tf_op jit(solution)/shard_map/all_gather | solution.py:34
  77.8 2.7 abs_bitcast_fusion
  80.5 2.4 copy.14
  82.9 3.1 reduce_max.9
  86.0 0.0 copy-start.1
  86.0 0.0 copy-start.2
  86.1 1.0 div.44
  87.1 0.5 copy-done.1
  87.5 0.6 copy-done.2
  88.1 0.0 copy-start.8
  88.1 0.0 copy-start.4
  88.1 0.0 copy-start.5
  88.1 4.3 fusion.3
  92.4 0.0 reduce-scatter.2.cloned.1.call-update
  92.4 0.2 all-gather.5.cloned.1.call-start
  92.7 0.5 all-gather.5.cloned.1.call-update
  93.2 0.0 copy-done.8
  93.2 0.1 slice.6
  93.3 0.1 slice.7
  93.4 51.1 %reduce-scatter.2.cloned.1.call-done = bf16[224,1024]{1,0:T(8,128)(2,1)} async-done(((bf16[224,4096]{1,0:T(8,128)(2,1)}), bf16[224,1024]{1,0:T(8,128)(2,1)}) %reduce-scatter.2.cloned.1.call-update) | async-done | bytes 458768 | tf_op jit(solution)/shard_map/reduce_scatter | solution.py:87
  144.6 0.0 copy-done.4
  144.6 0.0 copy-done.5
  144.6 2.4 subtract_convert_fusion
  146.9 64.6 %all-to-all-done = bf16[64,16,4096]{2,1,0:T(8,128)(2,1)} async-done(((bf16[64,16,4096]{2,1,0:T(8,128)(2,1)}), bf16[64,16,4096]{2,1,0:T(8,128)(2,1)}, u32[]{:S(2)}, u32[]{:S(2)}) %all-to-all-start) | async-done | bytes 8388640 | tf_op jit(solution)/shard_map/all_to_all | solution.py:17
  211.5 0.0 copy-start.3
  211.5 6.7 %fusion.6 = f32[1024,224]{0,1:T(8,128)S(1)} fusion(bf16[1024,4096]{1,0:T(8,128)(2,1)} %bitcast.1, bf16[1,224,4096]{2,1,0:T(8,128)(2,1)} %param.13), kind=kOutput, calls=%fused_computation.12 | convolution fusion | flops 1879048192 | bytes 11141120 | tf_op jit(solution)/shard_map/dot_general | solution.py:22
  218.2 0.0 copy-done.3
  218.2 0.0 copy-start.9
  218.2 0.0 copy-start.7
  218.2 7.4 %fusion.47 = f32[1024,224]{0,1:T(8,128)} fusion(bf16[1024,4096]{1,0:T(8,128)(2,1)} %bitcast.1, bf16[224,4096]{1,0:T(8,128)(2,1)S(1)} %copy-done.3), kind=kOutput, calls=%fused_computation.70 | convolution fusion | flops 1879048192 | bytes 11141120 | tf_op jit(solution)/shard_map/dot_general | solution.py:22
  225.6 0.0 copy-done.9
  225.6 0.0 copy-done
  225.6 0.0 copy-done.7
  225.6 7.0 %fusion.19 = (f32[1024]{0:T(1024)S(1)}, f32[1024,224]{0,1:T(8,128)}) fusion(bf16[1024,224]{0,1:T(8,128)(2,1)S(1)} %copy-done.7, f32[1024,224]{0,1:T(8,128)S(1)} %fusion.6, bf16[1024,4096]{1,0:T(8,128)(2,1)} %bitcast.1, bf16[1,224,4096]{2,1,0:T(8,128)(2,1)S(1)} %copy-done), kind=kOutput, calls=%fused_computation.32 | convolution fusion | flops 1881340928 | bytes 12521472 | tf_op jit(solution)/shard_map/dot_general | solution.py:22
  232.7 0.0 copy-start.6
  232.7 0.0 all-gather.5.cloned.1.call-done
  232.7 7.0 %fusion.10 = f32[1024]{0:T(1024)S(1)} fusion(bf16[1024,224]{0,1:T(8,128)(2,1)S(1)} %copy-done.7, bf16[1024,4096]{1,0:T(8,128)(2,1)} %bitcast.1, bf16[224,4096]{1,0:T(8,128)(2,1)} %all-gather.5.cloned.1.call-done, f32[1024,224]{0,1:T(8,128)} %fusion.47), kind=kOutput, calls=%fused_computation.20 | convolution fusion | flops 1881340928 | bytes 11603968 | tf_op jit(solution)/shard_map/dot_general | solution.py:22
  239.7 0.0 copy-done.6
  239.7 0.1 reshape.45
  239.8 0.1 reshape.46
  239.9 0.1 reduce_sum.46
  240.0 0.1 reduce_sum.48
  240.1 182.6 %all-reduce = (f32[64]{0:T(128)S(1)}, f32[64]{0:T(128)S(1)}) all-reduce(f32[64]{0:T(128)S(1)} %reduce_sum.46, f32[64]{0:T(128)S(1)} %reduce_sum.48), channel_id=1, replica_groups=mesh['rep'=4,'fsdp'=64] {'fsdp'}, use_global_device_ids=true, to_apply=%region_2.3 | all-reduce | flops 128 | bytes 1024 | tf_op jit(solution)/shard_map/psum | solution.py:49
  422.7 0.2 convolution_bitcast_fusion.2
  422.9 0.8 fusion.35
  423.7 0.2 convolution_bitcast_fusion
  423.9 0.1 broadcast_in_dim.6
  424.0 0.1 reshape.48
  424.1 0.0 copy-start.10
  424.1 0.0 copy-start.11
  424.1 7.2 %fusion.1 = bf16[1,224,4096]{2,1,0:T(8,128)(2,1)} fusion(bf16[1024,4096]{1,0:T(8,128)(2,1)} %bitcast.1, bf16[1024,224]{0,1:T(8,128)(2,1)S(1)} %copy-done.7, f32[1024]{0:T(1024)S(1)} %convert_multiply_fusion.4, f32[1024,224]{0,1:T(8,128)} %copy-done.9), kind=kOutput, calls=%fused_computation.3 | convolution fusion | flops 1881800704 | bytes 11603968 | tf_op jit(solution)/shard_map/dot_general | solution.py:77
  431.3 0.0 copy-done.10
  431.3 0.0 copy-done.11
  431.3 6.9 %fusion = bf16[1,224,4096]{2,1,0:T(8,128)(2,1)} fusion(bf16[1024,4096]{1,0:T(8,128)(2,1)} %bitcast.1, f32[1024,224]{0,1:T(8,128)S(1)} %copy-done.11, bf16[1024,224]{0,1:T(8,128)(2,1)S(1)} %copy-done.7, f32[1024,224]{0,1:T(8,128)S(1)} %copy-done.10, f32[1024]{0:T(1024)S(1)} %convert_multiply_fusion.4), kind=kOutput, calls=%fused_computation.2 | convolution fusion | flops 1882718208 | bytes 12521472 | tf_op jit(solution)/shard_map/dot_general | solution.py:74
  (3 shorter events, 0.0 us)
Async XLA Ops:
  7.2 218.5 %copy-start = (bf16[1,224,4096]{2,1,0:T(8,128)(2,1)S(1)}, bf16[1,224,4096]{2,1,0:T(8,128)(2,1)}, u32[]{:S(2)}) copy-start(bf16[1,224,4096]{2,1,0:T(8,128)(2,1)} %param.14) | copy-start | bytes 5505028
  12.5 199.0 %all-to-all-start = ((bf16[64,16,4096]{2,1,0:T(8,128)(2,1)}), bf16[64,16,4096]{2,1,0:T(8,128)(2,1)}, u32[]{:S(2)}, u32[]{:S(2)}) async-start(bf16[64,16,4096]{2,1,0:T(8,128)(2,1)} %stack.2), calls=%async_computation | async-start | bytes 16777216 | tf_op jit(solution)/shard_map/all_to_all | solution.py:17
  26.4 51.4 %all-gather.3.cloned.1.call-start = ((), (), s32[]{:S(2)}) async-start(), calls=%async_computation.2 | async-start | bytes 2293760 | tf_op jit(solution)/shard_map/all_gather | solution.py:34
  27.2 117.4 %reduce-scatter.2.cloned.1.call-start = ((), (), s32[]{:S(2)}) async-start(), calls=%async_computation.4 | async-start | bytes 2293760 | tf_op jit(solution)/shard_map/reduce_scatter | solution.py:87
  86.0 1.5 copy-start.1
  86.0 2.0 copy-start.2
  88.1 5.1 %copy-start.8 = (s32[1,64]{1,0:T(1,128)S(1)}, s32[1,64]{1,0:T(1,128)}, u32[]{:S(2)}) copy-start(s32[1,64]{1,0:T(1,128)} %param.12) | copy-start | bytes 772
  88.1 56.5 %copy-start.4 = (bf16[224,1024]{1,0:T(8,128)(2,1)S(1)}, bf16[224,1024]{1,0:T(8,128)(2,1)}, u32[]{:S(2)}) copy-start(bf16[224,1024]{1,0:T(8,128)(2,1)} %param.15) | copy-start | bytes 1376260
  88.1 56.5 %copy-start.5 = (f32[224,1024]{1,0:T(8,128)S(1)}, f32[224,1024]{1,0:T(8,128)}, u32[]{:S(2)}) copy-start(f32[224,1024]{1,0:T(8,128)} %param.17) | copy-start | bytes 2752516
  92.4 140.2 %all-gather.5.cloned.1.call-start = ((), (), s32[]{:S(2)}) async-start(), calls=%async_computation.3 | async-start | bytes 2293760 | tf_op jit(solution)/shard_map/all_gather | solution.py:35
  211.5 6.7 %copy-start.3 = (bf16[224,4096]{1,0:T(8,128)(2,1)S(1)}, bf16[224,4096]{1,0:T(8,128)(2,1)}, u32[]{:S(2)}) copy-start(bf16[224,4096]{1,0:T(8,128)(2,1)} %all-gather.3.cloned.1.call-done) | copy-start | bytes 5505028
  218.2 7.4 %copy-start.9 = (f32[1024,224]{0,1:T(8,128)}, f32[1024,224]{0,1:T(8,128)S(1)}, u32[]{:S(2)}) copy-start(f32[1024,224]{0,1:T(8,128)S(1)} %fusion.6) | copy-start | bytes 2752516
  218.2 7.4 %copy-start.7 = (bf16[1024,224]{0,1:T(8,128)(2,1)S(1)}, bf16[1024,224]{0,1:T(8,128)(2,1)}, u32[]{:S(2)}) copy-start(bf16[1024,224]{0,1:T(8,128)(2,1)} %param.10) | copy-start | bytes 1376260
  232.7 7.0 %copy-start.6 = (s32[1024]{0:T(1024)S(1)}, s32[1024]{0:T(1024)}, u32[]{:S(2)}) copy-start(s32[1024]{0:T(1024)} %param.11) | copy-start | bytes 12292
  424.1 7.2 %copy-start.10 = (f32[1024,224]{0,1:T(8,128)S(1)}, f32[1024,224]{0,1:T(8,128)}, u32[]{:S(2)}) copy-start(f32[1024,224]{0,1:T(8,128)} %copy-done.9) | copy-start | bytes 2752516
  424.1 7.2 %copy-start.11 = (f32[1024,224]{0,1:T(8,128)S(1)}, f32[1024,224]{0,1:T(8,128)}, u32[]{:S(2)}) copy-start(f32[1024,224]{0,1:T(8,128)} %get-tuple-element.12) | copy-start | bytes 2752516
Sparse Core Ops, SparseCore 0:
  29.1 48.6 all-gather.2
  92.6 51.9 reduce-scatter.1
  146.4 48.6 all-gather.4
